TPU v7x, 32 devices: a whole 2x2x4 slice. The times are simulated.
32 devices in a mesh: hap: 2 (over x), snp: 16 (over z, y, core).
Axes of the slice: x: 2, y: 2, z: 4, core: 2. Of those that a mesh axis runs over, the one named last changes fastest.
Arguments:
- packed_panel: int32 [96, 16384], P('hap', 'snp'), may hold values from 0 to 8191, as said below
- components: bfloat16 [64, 1248], P(None, 'hap'), may hold values from -0.15625 to 0.15625
- bounds: int32 [2, 16384], P(None, 'snp'), may hold values from 0 to 16383, as said below
- band_width: int32 [16384], P('snp'), may hold values from 1 to 256
Outputs:
- ld_scores: float32 [16384], P('snp')
Inputs may be any that keep to these rules, and one draw needn't show every extreme that they name: Bit j of packed_panel[w, s] (j from 0 to 12) is the allele of haplotype 13 w + j at SNP s; higher bits are zero. LD blocks are consecutive runs of 1 to 2048 SNPs that cover all SNPs in order; bounds[0, s] and bounds[1, s] are the first and last SNP of the block holding s.
All inputs are finite; a program needn't handle non-finite values.
Results may differ from a plain program's by a relative error of at most 0.00074.
Values may be sent and summed in bfloat16 or wider, within the bound.
No kernel may reach another device: no remote copies, remote signals or barrier semaphores. Data moves between devices by JAX's collectives and lax.ppermute only.
A program may use at most 64 MiB of HBM per device.

v0:
```python
import jax
import jax.numpy as jnp
from jax import lax
from jax.sharding import PartitionSpec as P

epsilon = 1e-06


def padded_2(block, sides, width):
    for axis, dim in sides:
        count = lax.axis_size(axis)
        forward = [(i, i + 1) for i in range(count - 1)]
        backward = [(target, source) for source, target in forward]
        low = lax.ppermute(
            lax.slice_in_dim(block, block.shape[dim] - width, None, axis=dim), axis, forward
        )
        high = lax.ppermute(lax.slice_in_dim(block, 0, width, axis=dim), axis, backward)
        block = jnp.concatenate([low, block, high], axis=dim)
    return block


def unpack(packed):
    shifts = jnp.arange(13, dtype=jnp.int32)
    bit_values = jnp.bitwise_and(jnp.right_shift(packed[:, None, :], shifts[None, :, None]), 1)
    return bit_values.reshape(packed.shape[0] * 13, packed.shape[1]).astype(jnp.bfloat16)


def project(components, packed_panel):
    column_count = packed_panel.shape[1]
    block_size = min(256, column_count)
    zeroed = jnp.zeros((components.shape[0], column_count), jnp.float32)

    def add_block(block_index, accumulated):
        packed = lax.dynamic_slice_in_dim(packed_panel, block_index * block_size, block_size, 1)
        product = jnp.dot(components, unpack(packed), preferred_element_type=jnp.float32)
        return lax.dynamic_update_slice_in_dim(accumulated, product, block_index * block_size, 1)

    return lax.fori_loop(0, column_count // block_size, add_block, zeroed)


def standardize(factor):
    average = jnp.mean(factor, axis=1, keepdims=True)
    centered = factor - average
    variance = jnp.mean(centered * centered, axis=1, keepdims=True)
    return (centered * lax.rsqrt(variance + epsilon)).astype(jnp.bfloat16)


def band_scores(padded, inverse, bounds, band_width, offset, start_row, row_count, reach_width):
    component_count = padded.shape[0]
    block_size = min(256, row_count)

    def block_scores(block_index):
        first_row = start_row + block_index * block_size
        row_part = lax.dynamic_slice_in_dim(padded, first_row + reach_width, block_size, 1)
        column_part = lax.dynamic_slice_in_dim(padded, first_row, block_size + 2 * reach_width, 1)
        inverse_rows = lax.dynamic_slice_in_dim(inverse, first_row + reach_width, block_size, 0)
        inverse_columns = lax.dynamic_slice_in_dim(
            inverse, first_row, block_size + 2 * reach_width, 0
        )
        block_first = lax.dynamic_slice_in_dim(bounds[0], first_row, block_size, 0)
        block_last = lax.dynamic_slice_in_dim(bounds[1], first_row, block_size, 0)
        row_reach = lax.dynamic_slice_in_dim(band_width, first_row, block_size, 0)
        inner_products = lax.dot_general(
            row_part, column_part, (((0,), (0,)), ((), ())), preferred_element_type=jnp.float32
        )
        correlation = (
            inner_products
            * (1.0 / component_count)
            * inverse_rows[:, None]
            * inverse_columns[None, :]
        )
        row_position = offset + first_row + jnp.arange(block_size, dtype=jnp.int32)
        column_position = (
            offset
            + first_row
            - reach_width
            + jnp.arange(block_size + 2 * reach_width, dtype=jnp.int32)
        )
        window_low = jnp.maximum(block_first, row_position - row_reach)
        window_high = jnp.minimum(block_last, row_position + row_reach)
        inside = (
            (column_position[None, :] >= window_low[:, None])
            & (column_position[None, :] <= window_high[:, None])
            & (column_position[None, :] != row_position[:, None])
        )
        squared_sum = jnp.sum(jnp.where(inside, correlation * correlation, 0.0), axis=1)
        window_count = jnp.sum(inside.astype(jnp.float32), axis=1)
        return component_count * squared_sum / jnp.maximum(window_count, 1.0)

    blocks = jnp.arange(row_count // block_size, dtype=jnp.int32)
    return lax.map(block_scores, blocks).reshape(row_count)


def on_device(packed_panel, components, bounds, band_width):
    partial_factor = project(components, packed_panel)
    column_count = partial_factor.shape[1]
    factor = lax.psum(partial_factor, "hap")
    component_rows = lax.all_to_all(factor, "snp", split_axis=0, concat_axis=1, tiled=True)
    scaled = standardize(component_rows)
    normed = lax.all_to_all(scaled, "snp", split_axis=1, concat_axis=0, tiled=True)
    reach_width = column_count // 4
    padded = padded_2(normed, (("snp", 1),), reach_width)
    inverse = lax.rsqrt(jnp.mean(jnp.square(padded.astype(jnp.float32)), axis=0) + epsilon)
    offset = lax.axis_index("snp") * column_count
    share_rows = column_count // lax.axis_size("hap")
    own_scores = band_scores(
        padded,
        inverse,
        bounds,
        band_width,
        offset,
        lax.axis_index("hap") * share_rows,
        share_rows,
        reach_width,
    )
    return lax.all_gather(own_scores, "hap", axis=0, tiled=True)


def solution(mesh):
    in_specs = (P("hap", "snp"), P(None, "hap"), P(None, "snp"), P("snp"))
    out_specs = P("snp")
    return jax.shard_map(
        on_device, mesh=mesh, in_specs=in_specs, out_specs=out_specs, check_vma=False
    )
```

profile of v0, /device:TPU:13, one launch (start us, length us, event | category | flops | bytes accessed | tf_op | source)
XLA Modules:
  0.0 91.0 jit_solution(2346714453307130350)
XLA Ops:
  6.5 0.0 all-reduce.2.cloned.1.call-start
  6.5 0.0 copy-start
  6.6 0.9 copy-done
  7.4 5.6 %while.25 = (s32[]{:T(128)}, f32[64,1024]{1,0:T(8,128)S(1)}, s32[48,1024]{1,0:T(8,128)}, bf16[64,624]{1,0:T(8,128)(2,1)S(1)}, s32[]{:T(128)}, /*index=5*/s32[]{:T(128)}, s32[]{:T(128)}, s32[]{:T(128)}) while((s32[]{:T(128)}, f32[64,1024]{1,0:T(8,128)S(1)}, s32[48,1024]{1,0:T(8,128)}, bf16[64,624]{1,0:T(8,128)(2,1)S(1)}, s32[]{:T(128)}, ...), condition=%wide.region_1.0_spmd, body=%wide.region_0.0_spmd.sunk | while | flops 20926468 | bytes 2862539 | solution.py:38
  7.4 0.8 constant_dynamic-slice_fusion.6
  8.2 0.1 shift_right_arithmetic.50
  8.3 0.1 shift_right_arithmetic.51
  8.4 0.1 shift_right_arithmetic.53
  8.5 0.3 fusion.22
  8.8 0.8 constant_dynamic-slice_fusion.6
  9.6 0.1 shift_right_arithmetic.50
  9.7 0.1 shift_right_arithmetic.51
  9.8 0.1 shift_right_arithmetic.53
  9.9 0.3 fusion.22
  10.3 0.8 constant_dynamic-slice_fusion.6
  11.1 0.1 shift_right_arithmetic.50
  11.1 0.1 shift_right_arithmetic.51
  11.2 0.1 shift_right_arithmetic.53
  11.4 0.3 fusion.22
  11.7 0.8 constant_dynamic-slice_fusion.6
  12.5 0.1 shift_right_arithmetic.50
  12.5 0.1 shift_right_arithmetic.51
  12.6 0.1 shift_right_arithmetic.53
  12.8 0.3 fusion.22
  13.1 0.8 all_to_all.22
  13.8 0.0 all-reduce.2.cloned.1.call-update
  13.9 24.1 %all-reduce.2.cloned.1.call-done = f32[16,4,1024]{2,1,0:T(4,128)} async-done(((f32[16,4,1024]{2,1,0:T(4,128)}), f32[16,4,1024]{2,1,0:T(4,128)}) %all-reduce.2.cloned.1.call-update) | async-done | bytes 262160 | tf_op jit(solution)/shard_map/psum | solution.py:97
  37.9 14.8 %all_to_all.29 = f32[16,4,1024]{2,1,0:T(4,128)S(1)} all-to-all(f32[16,4,1024]{2,1,0:T(4,128)} %all-reduce.2.cloned.1.call-done), channel_id=1, replica_groups=mesh['hap'=2,'snp'=16] {'snp'}, dimensions={0} | all-to-all | bytes 524288 | tf_op jit(solution)/shard_map/all_to_all | solution.py:98
  52.7 0.3 reduce_sum.51
  53.0 0.3 multiply_reduce_fusion.1
  53.3 0.1 fusion.11
  53.5 9.9 %all_to_all.30 = bf16[4,16,1024]{2,0,1:T(4,128)(2,1)S(1)} all-to-all(bf16[4,16,1024]{2,0,1:T(4,128)(2,1)S(1)} %fusion.11), channel_id=1, replica_groups=mesh['hap'=2,'snp'=16] {'snp'}, dimensions={1} | all-to-all | bytes 262144 | tf_op jit(solution)/shard_map/all_to_all | solution.py:100
  63.4 3.7 %collective-permute-start = (bf16[64,256]{1,0:T(8,128)(2,1)S(1)}, bf16[64,256]{1,0:T(8,128)(2,1)S(1)}, u32[]{:S(2)}, u32[]{:S(2)}) collective-permute-start(bf16[64,256]{1,0:T(8,128)(2,1)S(1)} %get-tuple-element.232), channel_id=1, source_target_pairs={{0,1},{1,2},{2,3},{3,4},{4,5},{5,6},{6,7},{7,8},{8,9},{9,10},{10,1... | collective-permute-start | bytes 98312 | tf_op jit(solution)/shard_map/ppermute | solution.py:14
  67.1 1.9 %collective-permute-start.1 = (bf16[64,256]{1,0:T(8,128)(2,1)S(1)}, bf16[64,256]{1,0:T(8,128)(2,1)S(1)}, u32[]{:S(2)}, u32[]{:S(2)}) collective-permute-start(bf16[64,256]{1,0:T(8,128)(2,1)S(1)} %get-tuple-element.231), channel_id=1, source_target_pairs={{1,0},{2,1},{3,2},{4,3},{5,4},{6,5},{7,6},{8,7},{9,8},{10,9},{11,1... | collective-permute-start | bytes 98312 | tf_op jit(solution)/shard_map/ppermute | solution.py:17
  69.1 0.0 collective-permute-done
  69.1 4.2 %collective-permute-done.1 = bf16[64,256]{1,0:T(8,128)(2,1)S(1)} collective-permute-done((bf16[64,256]{1,0:T(8,128)(2,1)S(1)}, bf16[64,256]{1,0:T(8,128)(2,1)S(1)}, u32[]{:S(2)}, u32[]{:S(2)}) %collective-permute-start.1) | collective-permute-done | bytes 32800 | tf_op jit(solution)/shard_map/ppermute | solution.py:17
  73.3 0.1 multiply_reduce_fusion
  73.3 0.0 copy-start.1
  73.4 0.7 copy-done.1
  74.0 6.3 %while.26 = (s32[]{:T(128)}, f32[2,256]{1,0:T(2,128)S(1)}, s32[2]{0:T(128)S(1)}, s32[]{:T(128)}, s32[]{:T(128)}, /*index=5*/s32[2,1024]{1,0:T(2,128)S(1)}, s32[1...) while((s32[]{:T(128)}, f32[2,256]{1,0:T(2,128)S(1)}, ...), condition=%wide.region_9.10_spmd, body=%wide.region_6.9_spmd.sunk | while | flops 28510736 | bytes 194922 | solution.py:91
  74.0 0.6 dynamic_slice.80
  75.4 0.8 subtract_maximum_fusion.2
  76.1 0.1 dynamic-slice_multiply_fusion.2
  76.2 0.1 dynamic_slice.81
  76.3 0.5 fusion.26
  76.8 0.3 convert_reduce_fusion.2
  77.2 0.6 dynamic_slice.80
  78.5 0.8 subtract_maximum_fusion.2
  79.3 0.1 dynamic-slice_multiply_fusion.2
  79.4 0.1 dynamic_slice.81
  79.5 0.5 fusion.26
  80.0 0.3 convert_reduce_fusion.2
  80.4 3.2 %all-gather = f32[2,1,512]{2,1,0:T(1,128)S(1)} all-gather(f32[1,1,512]{2,1,0:T(1,128)S(1)} %reshape.97), channel_id=1, replica_groups=mesh['hap'=2,'snp'=16] {'hap'}, dimensions={0}, use_global_device_ids=true | all-gather | bytes 6144 | tf_op jit(solution)/shard_map/all_gather | solution.py:116
  83.6 0.6 copy.23
  (28 shorter events, 0.3 us)
Async XLA Ops:
  6.5 31.4 %all-reduce.2.cloned.1.call-start = ((), (), s32[]{:S(2)}) async-start(), calls=%async_computation.2 | async-start | bytes 524288 | tf_op jit(solution)/shard_map/psum | solution.py:97
  6.5 0.9 copy-start
  63.4 5.7 %collective-permute-start = (bf16[64,256]{1,0:T(8,128)(2,1)S(1)}, bf16[64,256]{1,0:T(8,128)(2,1)S(1)}, u32[]{:S(2)}, u32[]{:S(2)}) collective-permute-start(bf16[64,256]{1,0:T(8,128)(2,1)S(1)} %get-tuple-element.232), channel_id=1, source_target_pairs={{0,1},{1,2},{2,3},{3,4},{4,5},{5,6},{6,7},{7,8},{8,9},{9,10},{10,1... | collective-permute-start | bytes 98312 | tf_op jit(solution)/shard_map/ppermute | solution.py:14
  67.1 6.1 %collective-permute-start.1 = (bf16[64,256]{1,0:T(8,128)(2,1)S(1)}, bf16[64,256]{1,0:T(8,128)(2,1)S(1)}, u32[]{:S(2)}, u32[]{:S(2)}) collective-permute-start(bf16[64,256]{1,0:T(8,128)(2,1)S(1)} %get-tuple-element.231), channel_id=1, source_target_pairs={{1,0},{2,1},{3,2},{4,3},{5,4},{6,5},{7,6},{8,7},{9,8},{10,9},{11,1... | collective-permute-start | bytes 98312 | tf_op jit(solution)/shard_map/ppermute | solution.py:17
  73.3 0.7 copy-start.1
Sparse Core Ops, SparseCore 0:
  14.0 23.8 all-reduce.1
where the time goes:
time: 91.7 us; the launch traced here: 91 us
  waiting for transfers between devices  28.2 us (31%)
  blocking collectives  27.9 us (30%)
  between operations  13.5 us (15%)
  local copies, waits for them, and re-layouts  8.78 us (10%)
  starting transfers between devices  5.62 us (6%)
  other arithmetic  3.17 us (3%)
  matrix products  2.22 us (2%)
  loops' own time  1.59 us (2%)
    psum x1, waiting for transfers between devices, on_device(): factor = lax.psum(partial_factor, 'hap')  24.1 us
    all_to_all x1, blocking collectives, on_device(): lax.all_to_all(factor, 'snp', split_axis=0, concat_axis=1, tiled=True)  14.8 us
    all_to_all x1, blocking collectives, on_device(): lax.all_to_all(scaled, 'snp', split_axis=1, concat_axis=0, tiled=True)  9.91 us
    ppermute x1, waiting for transfers between devices, padded_2(): lax.ppermute(lax.slice_in_dim(block, 0, width, axis=dim), axis, backward)  4.16 us
    ppermute x1, starting transfers between devices, padded_2(): lax.ppermute(lax.slice_in_dim(block, block.shape[dim] - width, None, axis...  3.7 us
    dynamic_slice x4, local copies, waits for them, and re-layouts, add_block(): lax.dynamic_slice_in_dim(packed_panel, block_index * block_size, block_si...  3.23 us
    all_gather x1, blocking collectives, on_device(): return lax.all_gather(own_scores, 'hap', axis=0, tiled=True)  3.21 us
    unnamed x8, local copies, waits for them, and re-layouts  2.16 us
  transfers between devices with their start and end apart: 3, of which 2 were waited for; matrix products, arithmetic and copies ran while one was open for 0% of the time, Pallas kernels for 0%

commit v1 on v0

v1 whole, which is shorter than its diff:
```python
import jax
import jax.numpy as jnp
from jax import lax
from jax.experimental import pallas as pl
from jax.experimental.pallas import tpu as pltpu
from jax.sharding import PartitionSpec as P

EPSILON = 1e-06
LANES = 128
SUBLANES = 8


def whole_in_vmem(count):
    return [pl.BlockSpec(memory_space=pltpu.VMEM)] * count


def project(components, packed_panel):
    rank, haps = components.shape
    words, columns = packed_panel.shape
    bits = haps // words

    def kernel(panel_ref, components_ref, out_ref, turned):
        turned[...] = components_ref[...].astype(jnp.float32).T
        weights = [turned[pl.ds(j, words, stride=bits), :] for j in range(bits)]
        weights = jnp.concatenate(weights, axis=0).astype(jnp.bfloat16)
        panel = panel_ref[...]
        alleles = [
            (jnp.right_shift(panel, j) & 1).astype(jnp.float32).astype(jnp.bfloat16)
            for j in range(bits)
        ]
        alleles = jnp.concatenate(alleles, axis=0)
        out_ref[...] = lax.dot_general(
            weights, alleles, (((0,), (0,)), ((), ())), preferred_element_type=jnp.float32
        )

    return pl.pallas_call(
        kernel,
        out_shape=jax.ShapeDtypeStruct((rank, columns), jnp.float32),
        in_specs=whole_in_vmem(2),
        out_specs=pl.BlockSpec(memory_space=pltpu.VMEM),
        scratch_shapes=[pltpu.VMEM((haps, rank), jnp.float32)],
        name="project",
    )(packed_panel, components)


def combine(own, other, reach):
    rank, columns = own.shape

    def kernel(own_ref, other_ref, factor_ref, near_ref, far_ref, moments_ref):
        odd = lax.rem(lax.axis_index("snp"), 2)
        factor = own_ref[...] + other_ref[...]
        factor_ref[...] = factor
        average = jnp.sum(factor, axis=1, keepdims=True) * (1.0 / columns)
        centered = factor - average
        deviation = jnp.sum(centered * centered, axis=1, keepdims=True)
        lane = lax.broadcasted_iota(jnp.int32, (rank, LANES), 1)
        moments_ref[...] = jnp.where(lane == 0, average, deviation).T[:SUBLANES]
        low = factor[:, :reach]
        high = factor[:, columns - reach :]
        near_ref[...] = jnp.where(odd == 1, low, high)
        far_ref[...] = jnp.where(odd == 1, high, low)

    edge = jax.ShapeDtypeStruct((rank, reach), jnp.float32)
    return pl.pallas_call(
        kernel,
        out_shape=(
            jax.ShapeDtypeStruct((rank, columns), jnp.float32),
            edge,
            edge,
            jax.ShapeDtypeStruct((SUBLANES, rank), jnp.float32),
        ),
        in_specs=whole_in_vmem(2),
        out_specs=tuple(whole_in_vmem(4)),
        name="combine",
    )(own, other)


def band_scores(factor, near, far, moments, bounds, band_width, total):
    rank, columns = factor.shape
    reach = near.shape[1]
    padded = columns + 2 * reach
    tile = LANES
    span = tile + 2 * reach

    def kernel(factor_ref, near_ref, far_ref, moments_ref, bounds_ref, width_ref, out_ref, turned, scale, normed_ref):
        place = lax.axis_index("snp")
        odd = lax.rem(place, 2)
        moments = jnp.concatenate([moments_ref[...]] * (LANES // rank), axis=1).T
        average = moments[:rank, 0:1]
        gain = lax.rsqrt(moments[:rank, 1:2] * (1.0 / total) + EPSILON)
        near, far = near_ref[...], far_ref[...]
        wide = jnp.concatenate(
            [jnp.where(odd == 1, near, far), factor_ref[...], jnp.where(odd == 1, far, near)], axis=1
        )
        normed = ((wide - average) * gain).astype(jnp.bfloat16)
        normed_ref[...] = normed
        exact = normed.astype(jnp.float32)
        squares = exact * exact
        inverse = lax.rsqrt(jnp.sum(squares, axis=0, keepdims=True) * (1.0 / rank) + EPSILON)
        turned[...] = exact.T.astype(jnp.bfloat16)
        upper = squares.astype(jnp.bfloat16)
        lower = (squares - upper.astype(jnp.float32)).astype(jnp.bfloat16)
        norms = lax.dot_general(
            jnp.concatenate([upper, lower], axis=0),
            jnp.ones((2 * rank, LANES), jnp.bfloat16),
            (((0,), (0,)), ((), ())),
            preferred_element_type=jnp.float32,
        )
        scale[...] = lax.rsqrt(norms * (1.0 / rank) + EPSILON)
        for first in range(0, columns, tile):
            position = first + lax.broadcasted_iota(jnp.int32, (1, tile), 1)
            width = width_ref[:, first : first + tile]
            start = bounds_ref[0:1, first : first + tile] - place * columns
            stop = bounds_ref[1:2, first : first + tile] - place * columns
            low = jnp.maximum(start, position - width)
            high = jnp.minimum(stop, position + width)
            low_in = low - (first - reach)
            high_in = high - (first - reach)
            rows = normed_ref[:, first + reach : first + reach + tile]
            products = jnp.dot(
                turned[first : first + span, :], rows, preferred_element_type=jnp.float32
            )
            products = products * scale[first : first + span, :]
            column = lax.broadcasted_iota(jnp.int32, (span, tile), 0)
            inside = (column >= low_in) & (column <= high_in)
            inside &= column != reach + lax.broadcasted_iota(jnp.int32, (span, tile), 1)
            summed = jnp.sum(jnp.where(inside, products * products, 0.0), axis=0, keepdims=True)
            own = inverse[:, first + reach : first + reach + tile]
            count = jnp.maximum(high - low, 1).astype(jnp.float32)
            out_ref[:, first : first + tile] = summed * (own * own) * (1.0 / rank) / count

    return pl.pallas_call(
        kernel,
        out_shape=jax.ShapeDtypeStruct((1, columns), jnp.float32),
        in_specs=whole_in_vmem(6),
        out_specs=pl.BlockSpec(memory_space=pltpu.VMEM),
        scratch_shapes=[
            pltpu.VMEM((padded, rank), jnp.bfloat16),
            pltpu.VMEM((padded, LANES), jnp.float32),
            pltpu.VMEM((rank, padded), jnp.bfloat16),
        ],
        name="band",
    )(factor, near, far, moments, bounds, band_width)


def swap(value, axis, distance):
    count = lax.axis_size(axis)
    return lax.ppermute(value, axis, [(i, i ^ distance) for i in range(count)])


def powers(count):
    steps = [1 << b for b in range(count.bit_length() - 1)]
    if 1 << len(steps) != count:
        raise ValueError("axis size")
    return steps


def on_device(packed_panel, components, bounds, band_width):
    columns = packed_panel.shape[1]
    reach = columns // 4
    devices = lax.axis_size("snp")
    partial = project(components, packed_panel)
    hap_steps = powers(lax.axis_size("hap"))
    for distance in hap_steps[:-1]:
        partial = partial + swap(partial, "hap", distance)
    other = swap(partial, "hap", hap_steps[-1])
    factor, near, far, moments = combine(partial, other, reach)
    outward = [(i, i + 1) for i in range(1, devices - 1, 2)]
    near = swap(near, "snp", 1)
    far = lax.ppermute(far, "snp", outward + [(j, i) for i, j in outward])
    row = lax.broadcasted_iota(jnp.int32, (SUBLANES, 1), 0)
    members = columns
    for distance in powers(devices):
        met = swap(moments, "snp", distance)
        gap = moments[0:1] - met[0:1]
        both = moments + met
        moments = jnp.where(row == 0, 0.5 * both, both + gap * gap * (0.5 * members))
        members *= 2
    scores = band_scores(factor, near, far, moments, bounds, band_width[None], members)
    return scores.reshape(columns)


def solution(mesh):
    in_specs = (P("hap", "snp"), P(None, "hap"), P(None, "snp"), P("snp"))
    return jax.shard_map(
        on_device, mesh=mesh, in_specs=in_specs, out_specs=P("snp"), check_vma=False
    )
```

time: 91.7 us -> 36.5 us (0.40)
  blocking collectives: 27.9 us -> 0 us
  between operations: 13.5 us -> 0.04 us
  waiting for transfers between devices: 28.2 us -> 15.8 us
  local copies, waits for them, and re-layouts: 8.78 us -> 1.33 us
  Pallas kernels: 0 us -> 7.24 us
  starting transfers between devices: 5.62 us -> 10.3 us
  matrix products: 2.22 us -> 0 us
  loops' own time: 1.59 us -> 0 us
  other arithmetic: 3.17 us -> 1.6 us
    all_to_all x2 -> x0, blocking collectives: 24.7 us -> none  [the longest x1 14.8 us: on_device(): lax.all_to_all(factor, 'snp', split_axis=0, concat_axis=1, tiled=True)]
    psum x1 -> x0, waiting for transfers between devices: 24.1 us -> none  [on_device(): factor = lax.psum(partial_factor, 'hap')]
    ppermute x2 -> x7, waiting for transfers between devices: 4.17 us -> 15.8 us  [the longest x6 11.7 us: swap(): return lax.ppermute(value, axis, [(i, i ^ distance) for i in range(count)])]
    pallas_call x0 -> x3, Pallas kernels: none -> 7.24 us  [the longest x1 3.1 us: band_scores(): pl.pallas_call(kernel, out_shape=jax.ShapeDtypeStruct((1, columns), jnp.f...]
    ppermute x2 -> x7, starting transfers between devices: 5.62 us -> 10.3 us  [the longest x6 8.37 us: swap(): return lax.ppermute(value, axis, [(i, i ^ distance) for i in range(count)])]
    dynamic_slice x12 -> x0, local copies, waits for them, and re-layouts: 4.64 us -> none  [the longest x4 3.23 us: add_block(): lax.dynamic_slice_in_dim(packed_panel, block_index * block_size, block_si...]
    all_gather x1 -> x0, blocking collectives: 3.21 us -> none  [on_device(): return lax.all_gather(own_scores, 'hap', axis=0, tiled=True)]
    dot_general x6 -> x0, matrix products: 2.22 us -> none  [the longest x4 1.16 us: add_block(): jnp.dot(components, unpack(packed), preferred_element_type=jnp.float32)]
  transfers between devices with their start and end apart: 3 -> 7, of which waited for: 2 -> 5; matrix products, arithmetic and copies ran while one was open for 0% -> 2% of each run, Pallas kernels for 0% -> 0%
where the time goes in v1:
time: 36.5 us; the launch traced here: 36.3 us
  waiting for transfers between devices  15.8 us (43%)
  starting transfers between devices  10.3 us (28%)
  Pallas kernels  7.24 us (20%)
  other arithmetic  1.6 us (4%)
  local copies, waits for them, and re-layouts  1.33 us (4%)
    ppermute x6, waiting for transfers between devices, swap(): return lax.ppermute(value, axis, [(i, i ^ distance) for i in range(count)])  11.7 us
    ppermute x6, starting transfers between devices, swap(): return lax.ppermute(value, axis, [(i, i ^ distance) for i in range(count)])  8.37 us
    ppermute x1, waiting for transfers between devices, on_device(): far = lax.ppermute(far, 'snp', outward + [(j, i) for i, j in outward])  4.07 us
    pallas_call x1, Pallas kernels, band_scores(): pl.pallas_call(kernel, out_shape=jax.ShapeDtypeStruct((1, columns), jnp.f...  3.1 us
    pallas_call x1, Pallas kernels, project(): pl.pallas_call(kernel, out_shape=jax.ShapeDtypeStruct((rank, columns), jn...  2.26 us
    ppermute x1, starting transfers between devices, on_device(): far = lax.ppermute(far, 'snp', outward + [(j, i) for i, j in outward])  1.91 us
    pallas_call x1, Pallas kernels, combine(): pl.pallas_call(kernel, out_shape=(jax.ShapeDtypeStruct((rank, columns), j...  1.88 us
    unnamed x8, local copies, waits for them, and re-layouts  1.33 us
  transfers between devices with their start and end apart: 7, of which 5 were waited for; matrix products, arithmetic and copies ran while one was open for 2% of the time, Pallas kernels for 0%

profile of v1, /device:TPU:13, one launch (start us, length us, event | category | flops | bytes accessed | tf_op | source)
XLA Modules:
  0.0 36.3 jit_solution(17357283612939247580)
XLA Ops:
  0.0 2.3 %project.1.own_ref = f32[64,1024]{1,0:T(8,128)} custom-call(s32[48,1024]{1,0:T(8,128)} %panel_ref.1, bf16[64,624]{1,0:T(8,128)(2,1)} %components_ref.1), custom_call_target="tpu_custom_call" | custom-call | tf_op jit(solution)/shard_map/project/pallas_call | solution.py:36
  2.3 1.2 %collective-permute-start = (f32[64,1024]{1,0:T(8,128)}, f32[64,1024]{1,0:T(8,128)S(1)}, u32[]{:S(2)}, u32[]{:S(2)}) collective-permute-start(f32[64,1024]{1,0:T(8,128)} %project.1.own_ref), channel_id=1, source_target_pairs={{0,16},{16,0},{1,17},{17,1},{2,18},{18,2},{3,19},{19,3},{4,20},{20... | collective-permute-start | bytes 786440 | tf_op jit(solution)/shard_map/ppermute | solution.py:148
  3.5 6.2 %collective-permute-done.other_ref = f32[64,1024]{1,0:T(8,128)S(1)} collective-permute-done((f32[64,1024]{1,0:T(8,128)}, f32[64,1024]{1,0:T(8,128)S(1)}, u32[]{:S(2)}, u32[]{:S(2)}) %collective-permute-start) | collective-permute-done | bytes 262176 | tf_op jit(solution)/shard_map/ppermute | solution.py:148
  9.7 0.0 copy-start
  9.7 0.7 %copy-done = f32[64,1024]{1,0:T(8,128)} copy-done((f32[64,1024]{1,0:T(8,128)}, f32[64,1024]{1,0:T(8,128)S(1)}, u32[]{:S(2)}) %copy-start) | copy-done | bytes 262168
  10.4 1.9 %combine.1 = (f32[64,1024]{1,0:T(8,128)}, f32[64,256]{1,0:T(8,128)}, f32[64,256]{1,0:T(8,128)}, f32[8,64]{1,0:T(8,128)}) custom-call(f32[64,1024]{1,0:T(8,128)} %project.1.own_ref, f32[64,1024]{1,0:T(8,128)} %copy-done), custom_call_target="tpu_custom_call" | custom-call | tf_op jit(solution)/shard_map/combine/pallas_call | solution.py:64
  12.2 0.0 copy-start.3
  12.2 1.5 %collective-permute-start.3 = (f32[8,64]{1,0:T(8,128)}, f32[8,64]{1,0:T(8,128)S(1)}, u32[]{:S(2)}, u32[]{:S(2)}) collective-permute-start(f32[8,64]{1,0:T(8,128)} %get-tuple-element.12), channel_id=1, source_target_pairs={{0,1},{1,0},{2,3},{3,2},{4,5},{5,4},{6,7},{7,6},{8,9},{9,8},{10,11... | collective-permute-start | bytes 6152 | tf_op jit(solution)/shard_map/ppermute | solution.py:148
  13.8 1.0 %collective-permute-done.3 = f32[8,64]{1,0:T(8,128)S(1)} collective-permute-done((f32[8,64]{1,0:T(8,128)}, f32[8,64]{1,0:T(8,128)S(1)}, u32[]{:S(2)}, u32[]{:S(2)}) %collective-permute-start.3) | collective-permute-done | bytes 2080 | tf_op jit(solution)/shard_map/ppermute | solution.py:148
  14.8 0.7 %multiply_bitcast_fusion.3 = f32[64]{0:T(128)S(1)} fusion(f32[8,64]{1,0:T(8,128)S(1)} %collective-permute-done.3, f32[8,64]{1,0:T(8,128)} %get-tuple-element.12), kind=kLoop, calls=%fused_computation.7 | loop fusion | flops 192 | bytes 768 | tf_op jit(solution)/shard_map/add | solution.py:177
  15.5 0.0 copy-done.3
  15.5 0.1 add_select_fusion.3
  15.6 0.2 collective-permute-start.4
  15.8 2.2 %collective-permute-done.4 = f32[8,64]{1,0:T(8,128)S(1)} collective-permute-done((f32[8,64]{1,0:T(8,128)S(1)}, f32[8,64]{1,0:T(8,128)S(1)}, u32[]{:S(2)}, u32[]{:S(2)}) %collective-permute-start.4) | collective-permute-done | bytes 2080 | tf_op jit(solution)/shard_map/ppermute | solution.py:148
  18.0 0.1 add_select_fusion.2
  18.1 0.2 collective-permute-start.5
  18.3 2.3 %collective-permute-done.5 = f32[8,64]{1,0:T(8,128)S(1)} collective-permute-done((f32[8,64]{1,0:T(8,128)S(1)}, f32[8,64]{1,0:T(8,128)S(1)}, u32[]{:S(2)}, u32[]{:S(2)}) %collective-permute-start.5) | collective-permute-done | bytes 2080 | tf_op jit(solution)/shard_map/ppermute | solution.py:148
  20.6 0.1 add_select_fusion.1
  20.7 2.3 %collective-permute-start.6 = (f32[8,64]{1,0:T(8,128)S(1)}, f32[8,64]{1,0:T(8,128)S(1)}, u32[]{:S(2)}, u32[]{:S(2)}) collective-permute-start(f32[8,64]{1,0:T(8,128)S(1)} %add_select_fusion.1), channel_id=1, source_target_pairs={{0,8},{1,9},{2,10},{3,11},{4,12},{5,13},{6,14},{7,15},{8,0},{9,1},... | collective-permute-start | bytes 6152 | tf_op jit(solution)/shard_map/ppermute | solution.py:148
  23.0 2.9 %collective-permute-start.1 = (f32[64,256]{1,0:T(8,128)}, f32[64,256]{1,0:T(8,128)S(1)}, u32[]{:S(2)}, u32[]{:S(2)}) collective-permute-start(f32[64,256]{1,0:T(8,128)} %get-tuple-element.10), channel_id=1, source_target_pairs={{0,1},{1,0},{2,3},{3,2},{4,5},{5,4},{6,7},{7,6},{8,9},{9,8},{10,11... | collective-permute-start | bytes 196616 | tf_op jit(solution)/shard_map/ppermute | solution.py:148
  25.9 1.9 %collective-permute-start.2 = (f32[64,256]{1,0:T(8,128)}, f32[64,256]{1,0:T(8,128)S(1)}, u32[]{:S(2)}, u32[]{:S(2)}) collective-permute-start(f32[64,256]{1,0:T(8,128)} %get-tuple-element.11), channel_id=1, source_target_pairs={{1,2},{3,4},{5,6},{7,8},{9,10},{11,12},{13,14},{2,1},{4,3},{6,5},{... | collective-permute-start | bytes 196616 | tf_op jit(solution)/shard_map/ppermute | solution.py:170
  27.8 0.0 collective-permute-done.6
  27.8 0.7 %add_select_fusion.moments_ref = f32[8,64]{1,0:T(8,128)} fusion(f32[8,64]{1,0:T(8,128)S(1)} %add_select_fusion.1, f32[8,64]{1,0:T(8,128)S(1)} %collective-permute-done.6, f32[64]{0:T(128)S(1)} %multiply_bitcast_fusion, pred[8]{0:T(512)(128)(4,1)S(1)} %iota_compare_fusion), kind=kLoop, calls=%fused_computation | loop fusion | flops 2048 | bytes 6408 | tf_op jit(solution)/shard_map/jit(_where)/select_n | solution.py:177
  28.5 0.0 collective-permute-done.1.near_ref
  28.5 0.0 copy-start.1
  28.5 4.1 %collective-permute-done.2.far_ref = f32[64,256]{1,0:T(8,128)S(1)} collective-permute-done((f32[64,256]{1,0:T(8,128)}, f32[64,256]{1,0:T(8,128)S(1)}, u32[]{:S(2)}, u32[]{:S(2)}) %collective-permute-start.2) | collective-permute-done | bytes 65568 | tf_op jit(solution)/shard_map/ppermute | solution.py:170
  32.6 0.0 copy-start.2
  32.6 0.0 copy-done.1
  32.6 0.6 %copy-done.2 = f32[64,256]{1,0:T(8,128)} copy-done((f32[64,256]{1,0:T(8,128)}, f32[64,256]{1,0:T(8,128)S(1)}, u32[]{:S(2)}) %copy-start.2) | copy-done | bytes 65560
  33.2 3.1 %band.1 = f32[1,1024]{1,0:T(1,128)} custom-call(f32[64,1024]{1,0:T(8,128)} %get-tuple-element.9.factor_ref, f32[64,256]{1,0:T(8,128)} %copy-done.1, f32[64,256]{1,0:T(8,128)} %copy-done.2, f32[8,64]{1,0:T(8,128)} %add_select_fusion.moments_ref, s32[2,1024]{1,0:T(2,128)} %bounds_ref.1, s32[1,1024]{1,0:T(1,128)} %bitcast.10), custom_call_target="tpu_custom_call" | custom-call | tf_op jit(solution)/shard_map/band/pallas_call | solution.py:132
  (4 shorter events, 0.0 us)
Async XLA Ops:
  2.3 7.4 %collective-permute-start = (f32[64,1024]{1,0:T(8,128)}, f32[64,1024]{1,0:T(8,128)S(1)}, u32[]{:S(2)}, u32[]{:S(2)}) collective-permute-start(f32[64,1024]{1,0:T(8,128)} %project.1.own_ref), channel_id=1, source_target_pairs={{0,16},{16,0},{1,17},{17,1},{2,18},{18,2},{3,19},{19,3},{4,20},{20... | collective-permute-start | bytes 786440 | tf_op jit(solution)/shard_map/ppermute | solution.py:148
  9.7 0.7 %copy-start = (f32[64,1024]{1,0:T(8,128)}, f32[64,1024]{1,0:T(8,128)S(1)}, u32[]{:S(2)}) copy-start(f32[64,1024]{1,0:T(8,128)S(1)} %collective-permute-done.other_ref) | copy-start | bytes 786436
  12.2 3.3 %copy-start.3 = (f32[8,64]{1,0:T(8,128)S(1)}, f32[8,64]{1,0:T(8,128)}, u32[]{:S(2)}) copy-start(f32[8,64]{1,0:T(8,128)} %get-tuple-element.12) | copy-start | bytes 6148
  12.2 2.6 %collective-permute-start.3 = (f32[8,64]{1,0:T(8,128)}, f32[8,64]{1,0:T(8,128)S(1)}, u32[]{:S(2)}, u32[]{:S(2)}) collective-permute-start(f32[8,64]{1,0:T(8,128)} %get-tuple-element.12), channel_id=1, source_target_pairs={{0,1},{1,0},{2,3},{3,2},{4,5},{5,4},{6,7},{7,6},{8,9},{9,8},{10,11... | collective-permute-start | bytes 6152 | tf_op jit(solution)/shard_map/ppermute | solution.py:148
  15.6 2.5 %collective-permute-start.4 = (f32[8,64]{1,0:T(8,128)S(1)}, f32[8,64]{1,0:T(8,128)S(1)}, u32[]{:S(2)}, u32[]{:S(2)}) collective-permute-start(f32[8,64]{1,0:T(8,128)S(1)} %add_select_fusion.3), channel_id=1, source_target_pairs={{0,2},{1,3},{2,0},{3,1},{4,6},{5,7},{6,4},{7,5},{8,10},{9,11},{10,... | collective-permute-start | bytes 6152 | tf_op jit(solution)/shard_map/ppermute | solution.py:148
  18.1 2.5 %collective-permute-start.5 = (f32[8,64]{1,0:T(8,128)S(1)}, f32[8,64]{1,0:T(8,128)S(1)}, u32[]{:S(2)}, u32[]{:S(2)}) collective-permute-start(f32[8,64]{1,0:T(8,128)S(1)} %add_select_fusion.2), channel_id=1, source_target_pairs={{0,4},{1,5},{2,6},{3,7},{4,0},{5,1},{6,2},{7,3},{8,12},{9,13},{10,... | collective-permute-start | bytes 6152 | tf_op jit(solution)/shard_map/ppermute | solution.py:148
  20.7 7.2 %collective-permute-start.6 = (f32[8,64]{1,0:T(8,128)S(1)}, f32[8,64]{1,0:T(8,128)S(1)}, u32[]{:S(2)}, u32[]{:S(2)}) collective-permute-start(f32[8,64]{1,0:T(8,128)S(1)} %add_select_fusion.1), channel_id=1, source_target_pairs={{0,8},{1,9},{2,10},{3,11},{4,12},{5,13},{6,14},{7,15},{8,0},{9,1},... | collective-permute-start | bytes 6152 | tf_op jit(solution)/shard_map/ppermute | solution.py:148
  23.0 5.5 %collective-permute-start.1 = (f32[64,256]{1,0:T(8,128)}, f32[64,256]{1,0:T(8,128)S(1)}, u32[]{:S(2)}, u32[]{:S(2)}) collective-permute-start(f32[64,256]{1,0:T(8,128)} %get-tuple-element.10), channel_id=1, source_target_pairs={{0,1},{1,0},{2,3},{3,2},{4,5},{5,4},{6,7},{7,6},{8,9},{9,8},{10,11... | collective-permute-start | bytes 196616 | tf_op jit(solution)/shard_map/ppermute | solution.py:148
  25.9 6.7 %collective-permute-start.2 = (f32[64,256]{1,0:T(8,128)}, f32[64,256]{1,0:T(8,128)S(1)}, u32[]{:S(2)}, u32[]{:S(2)}) collective-permute-start(f32[64,256]{1,0:T(8,128)} %get-tuple-element.11), channel_id=1, source_target_pairs={{1,2},{3,4},{5,6},{7,8},{9,10},{11,12},{13,14},{2,1},{4,3},{6,5},{... | collective-permute-start | bytes 196616 | tf_op jit(solution)/shard_map/ppermute | solution.py:170
  28.5 4.1 %copy-start.1 = (f32[64,256]{1,0:T(8,128)}, f32[64,256]{1,0:T(8,128)S(1)}, u32[]{:S(2)}) copy-start(f32[64,256]{1,0:T(8,128)S(1)} %collective-permute-done.1.near_ref) | copy-start | bytes 196612
  32.6 0.6 %copy-start.2 = (f32[64,256]{1,0:T(8,128)}, f32[64,256]{1,0:T(8,128)S(1)}, u32[]{:S(2)}) copy-start(f32[64,256]{1,0:T(8,128)S(1)} %collective-permute-done.2.far_ref) | copy-start | bytes 196612

commit v2 on v1

--- a/solution.py
+++ b/solution.py
@@ -5,9 +5,11 @@
 from jax.experimental.pallas import tpu as pltpu
 from jax.sharding import PartitionSpec as P
 
+
 EPSILON = 1e-06
 LANES = 128
 SUBLANES = 8
+BLOCK = 256
 
 
 def whole_in_vmem(count):
@@ -19,28 +21,67 @@
     words, columns = packed_panel.shape
     bits = haps // words
 
-    def kernel(panel_ref, components_ref, out_ref, turned):
-        turned[...] = components_ref[...].astype(jnp.float32).T
+    def kernel(panel_ref, components_ref, out_ref, panel, weights_in, turned, arrived):
+        copies = [
+            pltpu.make_async_copy(components_ref, weights_in, arrived.at[0]),
+            pltpu.make_async_copy(panel_ref, panel, arrived.at[1]),
+        ]
+        for copy in copies:
+            copy.start()
+        copies[0].wait()
+        turned[...] = weights_in[...].astype(jnp.float32).T
         weights = [turned[pl.ds(j, words, stride=bits), :] for j in range(bits)]
-        weights = jnp.concatenate(weights, axis=0).astype(jnp.bfloat16)
-        panel = panel_ref[...]
-        alleles = [
-            (jnp.right_shift(panel, j) & 1).astype(jnp.float32).astype(jnp.bfloat16)
-            for j in range(bits)
-        ]
-        alleles = jnp.concatenate(alleles, axis=0)
-        out_ref[...] = lax.dot_general(
-            weights, alleles, (((0,), (0,)), ((), ())), preferred_element_type=jnp.float32
-        )
+        weights = jnp.concatenate(weights, axis=0).T.astype(jnp.bfloat16)
+        copies[1].wait()
+        step = min(BLOCK, columns)
+        for first in range(0, columns, step):
+            packed = panel[:, first : first + step]
+            alleles = [
+                (jnp.right_shift(packed, j) & 1).astype(jnp.float32).astype(jnp.bfloat16)
+                for j in range(bits)
+            ]
+            out_ref[:, first : first + step] = jnp.dot(
+                weights, jnp.concatenate(alleles, axis=0), preferred_element_type=jnp.float32
+            )
 
     return pl.pallas_call(
         kernel,
         out_shape=jax.ShapeDtypeStruct((rank, columns), jnp.float32),
+        in_specs=[pl.BlockSpec(memory_space=pltpu.HBM)] * 2,
+        out_specs=pl.BlockSpec(memory_space=pltpu.VMEM),
+        scratch_shapes=[
+            pltpu.VMEM((words, columns), jnp.int32),
+            pltpu.VMEM((rank, haps), jnp.bfloat16),
+            pltpu.VMEM((haps, rank), jnp.float32),
+            pltpu.SemaphoreType.DMA((2,)),
+        ],
+        compiler_params=pltpu.CompilerParams(vmem_limit_bytes=8 << 20),
+        name="project",
+    )(
+        pltpu.with_memory_space_constraint(packed_panel, pltpu.HBM),
+        pltpu.with_memory_space_constraint(components, pltpu.HBM),
+    )
+
+
+def windows(bounds, band_width):
+    columns = bounds.shape[1]
+
+    def kernel(bounds_ref, width_ref, low_ref, high_ref):
+        offset = lax.axis_index("snp") * columns
+        position = lax.broadcasted_iota(jnp.int32, (1, columns), 1)
+        width = width_ref[...]
+        low_ref[...] = jnp.maximum(bounds_ref[0:1] - offset, position - width)
+        high_ref[...] = jnp.minimum(bounds_ref[1:2] - offset, position + width)
+
+    edge = jax.ShapeDtypeStruct((1, columns), jnp.int32)
+    return pl.pallas_call(
+        kernel,
+        out_shape=(edge, edge),
         in_specs=whole_in_vmem(2),
-        out_specs=pl.BlockSpec(memory_space=pltpu.VMEM),
-        scratch_shapes=[pltpu.VMEM((haps, rank), jnp.float32)],
-        name="project",
-    )(packed_panel, components)
+        out_specs=tuple(whole_in_vmem(2)),
+        compiler_params=pltpu.CompilerParams(vmem_limit_bytes=2 << 20),
+        name="windows",
+    )(bounds, band_width)
 
 
 def combine(own, other, reach):
@@ -71,18 +112,19 @@
         ),
         in_specs=whole_in_vmem(2),
         out_specs=tuple(whole_in_vmem(4)),
+        compiler_params=pltpu.CompilerParams(vmem_limit_bytes=4 << 20),
         name="combine",
     )(own, other)
 
 
-def band_scores(factor, near, far, moments, bounds, band_width, total):
+def band_scores(factor, near, far, moments, low, high, total):
     rank, columns = factor.shape
     reach = near.shape[1]
     padded = columns + 2 * reach
     tile = LANES
     span = tile + 2 * reach
 
-    def kernel(factor_ref, near_ref, far_ref, moments_ref, bounds_ref, width_ref, out_ref, turned, scale, normed_ref):
+    def kernel(factor_ref, near_ref, far_ref, moments_ref, low_ref, high_ref, out_ref, turned, scale, normed_ref):
         place = lax.axis_index("snp")
         odd = lax.rem(place, 2)
         moments = jnp.concatenate([moments_ref[...]] * (LANES // rank), axis=1).T
@@ -108,12 +150,8 @@
         )
         scale[...] = lax.rsqrt(norms * (1.0 / rank) + EPSILON)
         for first in range(0, columns, tile):
-            position = first + lax.broadcasted_iota(jnp.int32, (1, tile), 1)
-            width = width_ref[:, first : first + tile]
-            start = bounds_ref[0:1, first : first + tile] - place * columns
-            stop = bounds_ref[1:2, first : first + tile] - place * columns
-            low = jnp.maximum(start, position - width)
-            high = jnp.minimum(stop, position + width)
+            low = low_ref[:, first : first + tile]
+            high = high_ref[:, first : first + tile]
             low_in = low - (first - reach)
             high_in = high - (first - reach)
             rows = normed_ref[:, first + reach : first + reach + tile]
@@ -139,8 +177,9 @@
             pltpu.VMEM((padded, LANES), jnp.float32),
             pltpu.VMEM((rank, padded), jnp.bfloat16),
         ],
+        compiler_params=pltpu.CompilerParams(vmem_limit_bytes=8 << 20),
         name="band",
-    )(factor, near, far, moments, bounds, band_width)
+    )(factor, near, far, moments, low, high)
 
 
 def swap(value, axis, distance):
@@ -155,11 +194,21 @@
     return steps
 
 
+def merge(groups, members):
+    row = lax.broadcasted_iota(jnp.int32, groups[0].shape, 0)
+    total = sum(groups[1:], groups[0])
+    average = total[0:1] * (1.0 / len(groups))
+    gaps = [group[0:1] - average for group in groups]
+    spread = sum([gap * gap for gap in gaps[1:]], gaps[0] * gaps[0])
+    return jnp.where(row == 0, total * (1.0 / len(groups)), total + spread * float(members))
+
+
 def on_device(packed_panel, components, bounds, band_width):
     columns = packed_panel.shape[1]
     reach = columns // 4
     devices = lax.axis_size("snp")
     partial = project(components, packed_panel)
+    low, high = windows(bounds, band_width[None])
     hap_steps = powers(lax.axis_size("hap"))
     for distance in hap_steps[:-1]:
         partial = partial + swap(partial, "hap", distance)
@@ -168,15 +217,16 @@
     outward = [(i, i + 1) for i in range(1, devices - 1, 2)]
     near = swap(near, "snp", 1)
     far = lax.ppermute(far, "snp", outward + [(j, i) for i, j in outward])
-    row = lax.broadcasted_iota(jnp.int32, (SUBLANES, 1), 0)
+    steps = powers(devices)
+    rounds = [steps[:2]] + [[step] for step in steps[2:]]
     members = columns
-    for distance in powers(devices):
-        met = swap(moments, "snp", distance)
-        gap = moments[0:1] - met[0:1]
-        both = moments + met
-        moments = jnp.where(row == 0, 0.5 * both, both + gap * gap * (0.5 * members))
-        members *= 2
-    scores = band_scores(factor, near, far, moments, bounds, band_width[None], members)
+    for round_steps in rounds:
+        groups = [moments]
+        for distance in range(round_steps[0], 2 * round_steps[-1], round_steps[0]):
+            groups.append(swap(moments, "snp", distance))
+        moments = merge(groups, members)
+        members *= len(groups)
+    scores = band_scores(factor, near, far, moments, low, high, members)
     return scores.reshape(columns)
 
 

time: 36.5 us -> 30.5 us (0.84)
  the two profiles are of different devices: /device:TPU:13 before, /device:TPU:1 now
where the time goes in v2:
time: 30.5 us; the launch traced here: 30.4 us
  waiting for transfers between devices  13.3 us (44%)
  starting transfers between devices  12.6 us (41%)
  Pallas kernels  3.98 us (13%)
  other arithmetic  0.41 us (1%)
    ppermute x7, starting transfers between devices, swap(): return lax.ppermute(value, axis, [(i, i ^ distance) for i in range(count)])  10.5 us
    ppermute x7, waiting for transfers between devices, swap(): return lax.ppermute(value, axis, [(i, i ^ distance) for i in range(count)])  9.98 us
    ppermute x1, waiting for transfers between devices, on_device(): far = lax.ppermute(far, 'snp', outward + [(j, i) for i, j in outward])  3.28 us
    ppermute x1, starting transfers between devices, on_device(): far = lax.ppermute(far, 'snp', outward + [(j, i) for i, j in outward])  2.11 us
    pallas_call x1, Pallas kernels, band_scores(): pl.pallas_call(kernel, out_shape=jax.ShapeDtypeStruct((1, columns), jnp.f...  2.09 us
    pallas_call x1, Pallas kernels, project(): pl.pallas_call(kernel, out_shape=jax.ShapeDtypeStruct((rank, columns), jn...  1.63 us
  transfers between devices with their start and end apart: 8, of which 5 were waited for; matrix products, arithmetic and copies ran while one was open for 1% of the time, Pallas kernels for 0%

profile of v2, /device:TPU:1, one launch (start us, length us, event | category | flops | bytes accessed | tf_op | source)
XLA Modules:
  0.0 30.4 jit_solution(12008704177389170417)
XLA Ops:
  0.0 1.6 %project.1.own_ref = f32[64,1024]{1,0:T(8,128)S(1)} custom-call(s32[48,1024]{1,0:T(8,128)} %panel_ref.1, bf16[64,624]{1,0:T(8,128)(2,1)} %components_ref.1), custom_call_target="tpu_custom_call" | custom-call | tf_op jit(solution)/shard_map/project/pallas_call | solution.py:47
  1.6 2.1 %collective-permute-start = (f32[64,1024]{1,0:T(8,128)S(1)}, f32[64,1024]{1,0:T(8,128)S(1)}, u32[]{:S(2)}, u32[]{:S(2)}) collective-permute-start(f32[64,1024]{1,0:T(8,128)S(1)} %project.1.own_ref), channel_id=1, source_target_pairs={{0,16},{16,0},{1,17},{17,1},{2,18},{18,2},{3,19},{19,3},{4,20},{20... | collective-permute-start | bytes 786440 | tf_op jit(solution)/shard_map/ppermute | solution.py:187
  3.7 6.0 %collective-permute-done.other_ref = f32[64,1024]{1,0:T(8,128)S(1)} collective-permute-done((f32[64,1024]{1,0:T(8,128)S(1)}, f32[64,1024]{1,0:T(8,128)S(1)}, u32[]{:S(2)}, u32[]{:S(2)}) %collective-permute-start) | collective-permute-done | bytes 262176 | tf_op jit(solution)/shard_map/ppermute | solution.py:187
  9.7 0.3 combine.1
  10.0 1.3 %collective-permute-start.3 = (f32[8,64]{1,0:T(8,128)S(1)}, f32[8,64]{1,0:T(8,128)S(1)}, u32[]{:S(2)}, u32[]{:S(2)}) collective-permute-start(f32[8,64]{1,0:T(8,128)S(1)} %get-tuple-element.14), channel_id=1, source_target_pairs={{0,1},{1,0},{2,3},{3,2},{4,5},{5,4},{6,7},{7,6},{8,9},{9,8},{10,11... | collective-permute-start | bytes 6152 | tf_op jit(solution)/shard_map/ppermute | solution.py:187
  11.3 1.5 %collective-permute-start.4 = (f32[8,64]{1,0:T(8,128)S(1)}, f32[8,64]{1,0:T(8,128)S(1)}, u32[]{:S(2)}, u32[]{:S(2)}) collective-permute-start(f32[8,64]{1,0:T(8,128)S(1)} %get-tuple-element.14), channel_id=1, source_target_pairs={{0,2},{1,3},{2,0},{3,1},{4,6},{5,7},{6,4},{7,5},{8,10},{9,11},{10,... | collective-permute-start | bytes 6152 | tf_op jit(solution)/shard_map/ppermute | solution.py:187
  12.7 0.2 collective-permute-start.5
  13.0 0.0 collective-permute-done.3
  13.0 0.8 %collective-permute-done.4 = f32[8,64]{1,0:T(8,128)S(1)} collective-permute-done((f32[8,64]{1,0:T(8,128)S(1)}, f32[8,64]{1,0:T(8,128)S(1)}, u32[]{:S(2)}, u32[]{:S(2)}) %collective-permute-start.4) | collective-permute-done | bytes 2080 | tf_op jit(solution)/shard_map/ppermute | solution.py:187
  13.7 2.0 %collective-permute-done.5 = f32[8,64]{1,0:T(8,128)S(1)} collective-permute-done((f32[8,64]{1,0:T(8,128)S(1)}, f32[8,64]{1,0:T(8,128)S(1)}, u32[]{:S(2)}, u32[]{:S(2)}) %collective-permute-start.5) | collective-permute-done | bytes 2080 | tf_op jit(solution)/shard_map/ppermute | solution.py:187
  15.8 0.1 add_select_fusion.2
  15.9 1.3 %collective-permute-start.6 = (f32[8,64]{1,0:T(8,128)S(1)}, f32[8,64]{1,0:T(8,128)S(1)}, u32[]{:S(2)}, u32[]{:S(2)}) collective-permute-start(f32[8,64]{1,0:T(8,128)S(1)} %add_select_fusion.2), channel_id=1, source_target_pairs={{0,4},{1,5},{2,6},{3,7},{4,0},{5,1},{6,2},{7,3},{8,12},{9,13},{10,... | collective-permute-start | bytes 6152 | tf_op jit(solution)/shard_map/ppermute | solution.py:187
  17.2 1.2 %collective-permute-done.6 = f32[8,64]{1,0:T(8,128)S(1)} collective-permute-done((f32[8,64]{1,0:T(8,128)S(1)}, f32[8,64]{1,0:T(8,128)S(1)}, u32[]{:S(2)}, u32[]{:S(2)}) %collective-permute-start.6) | collective-permute-done | bytes 2080 | tf_op jit(solution)/shard_map/ppermute | solution.py:187
  18.3 0.1 fusion.1
  18.4 0.0 copy-start
  18.4 0.0 copy-start.1
  18.4 0.1 add_select_fusion.1
  18.5 2.3 %collective-permute-start.7 = (f32[8,64]{1,0:T(8,128)S(1)}, f32[8,64]{1,0:T(8,128)S(1)}, u32[]{:S(2)}, u32[]{:S(2)}) collective-permute-start(f32[8,64]{1,0:T(8,128)S(1)} %add_select_fusion.1), channel_id=1, source_target_pairs={{0,8},{1,9},{2,10},{3,11},{4,12},{5,13},{6,14},{7,15},{8,0},{9,1},... | collective-permute-start | bytes 6152 | tf_op jit(solution)/shard_map/ppermute | solution.py:187
  20.8 0.0 copy-done
  20.8 0.0 copy-done.1
  20.8 1.9 %collective-permute-start.1 = (f32[64,256]{1,0:T(8,128)S(1)}, f32[64,256]{1,0:T(8,128)S(1)}, u32[]{:S(2)}, u32[]{:S(2)}) collective-permute-start(f32[64,256]{1,0:T(8,128)S(1)} %get-tuple-element.12), channel_id=1, source_target_pairs={{0,1},{1,0},{2,3},{3,2},{4,5},{5,4},{6,7},{7,6},{8,9},{9,8},{10,11... | collective-permute-start | bytes 196616 | tf_op jit(solution)/shard_map/ppermute | solution.py:187
  22.7 2.1 %collective-permute-start.2 = (f32[64,256]{1,0:T(8,128)S(1)}, f32[64,256]{1,0:T(8,128)S(1)}, u32[]{:S(2)}, u32[]{:S(2)}) collective-permute-start(f32[64,256]{1,0:T(8,128)S(1)} %get-tuple-element.13), channel_id=1, source_target_pairs={{1,2},{3,4},{5,6},{7,8},{9,10},{11,12},{13,14},{2,1},{4,3},{6,5},{... | collective-permute-start | bytes 196616 | tf_op jit(solution)/shard_map/ppermute | solution.py:219
  24.8 0.0 collective-permute-done.7
  24.8 0.1 fusion
  24.9 0.1 add_select_fusion.moments_ref
  25.0 0.0 collective-permute-done.1.near_ref
  25.0 3.3 %collective-permute-done.2.far_ref = f32[64,256]{1,0:T(8,128)S(1)} collective-permute-done((f32[64,256]{1,0:T(8,128)S(1)}, f32[64,256]{1,0:T(8,128)S(1)}, u32[]{:S(2)}, u32[]{:S(2)}) %collective-permute-start.2) | collective-permute-done | bytes 65568 | tf_op jit(solution)/shard_map/ppermute | solution.py:219
  28.3 2.1 %band.1 = f32[1,1024]{1,0:T(1,128)} custom-call(f32[64,1024]{1,0:T(8,128)S(1)} %get-tuple-element.11.factor_ref, f32[64,256]{1,0:T(8,128)S(1)} %collective-permute-done.1.near_ref, f32[64,256]{1,0:T(8,128)S(1)} %collective-permute-done.2.far_ref, f32[8,64]{1,0:T(8,128)S(1)} %add_select_fusion.moments_ref, s32[1,1024]{1,0:T(1,128)S(1)} %get-tuple-element.15.low_ref, ...), custom_call_target="tpu_custom_call" | custom-call | tf_op jit(solution)/shard_map/band/pallas_call | solution.py:170
  (6 shorter events, 0.1 us)
Async XLA Ops:
  1.6 8.1 %collective-permute-start = (f32[64,1024]{1,0:T(8,128)S(1)}, f32[64,1024]{1,0:T(8,128)S(1)}, u32[]{:S(2)}, u32[]{:S(2)}) collective-permute-start(f32[64,1024]{1,0:T(8,128)S(1)} %project.1.own_ref), channel_id=1, source_target_pairs={{0,16},{16,0},{1,17},{17,1},{2,18},{18,2},{3,19},{19,3},{4,20},{20... | collective-permute-start | bytes 786440 | tf_op jit(solution)/shard_map/ppermute | solution.py:187
  10.0 3.0 %collective-permute-start.3 = (f32[8,64]{1,0:T(8,128)S(1)}, f32[8,64]{1,0:T(8,128)S(1)}, u32[]{:S(2)}, u32[]{:S(2)}) collective-permute-start(f32[8,64]{1,0:T(8,128)S(1)} %get-tuple-element.14), channel_id=1, source_target_pairs={{0,1},{1,0},{2,3},{3,2},{4,5},{5,4},{6,7},{7,6},{8,9},{9,8},{10,11... | collective-permute-start | bytes 6152 | tf_op jit(solution)/shard_map/ppermute | solution.py:187
  11.3 2.5 %collective-permute-start.4 = (f32[8,64]{1,0:T(8,128)S(1)}, f32[8,64]{1,0:T(8,128)S(1)}, u32[]{:S(2)}, u32[]{:S(2)}) collective-permute-start(f32[8,64]{1,0:T(8,128)S(1)} %get-tuple-element.14), channel_id=1, source_target_pairs={{0,2},{1,3},{2,0},{3,1},{4,6},{5,7},{6,4},{7,5},{8,10},{9,11},{10,... | collective-permute-start | bytes 6152 | tf_op jit(solution)/shard_map/ppermute | solution.py:187
  12.7 3.0 %collective-permute-start.5 = (f32[8,64]{1,0:T(8,128)S(1)}, f32[8,64]{1,0:T(8,128)S(1)}, u32[]{:S(2)}, u32[]{:S(2)}) collective-permute-start(f32[8,64]{1,0:T(8,128)S(1)} %get-tuple-element.14), channel_id=1, source_target_pairs={{0,3},{1,2},{2,1},{3,0},{4,7},{5,6},{6,5},{7,4},{8,11},{9,10},{10,... | collective-permute-start | bytes 6152 | tf_op jit(solution)/shard_map/ppermute | solution.py:187
  15.9 2.5 %collective-permute-start.6 = (f32[8,64]{1,0:T(8,128)S(1)}, f32[8,64]{1,0:T(8,128)S(1)}, u32[]{:S(2)}, u32[]{:S(2)}) collective-permute-start(f32[8,64]{1,0:T(8,128)S(1)} %add_select_fusion.2), channel_id=1, source_target_pairs={{0,4},{1,5},{2,6},{3,7},{4,0},{5,1},{6,2},{7,3},{8,12},{9,13},{10,... | collective-permute-start | bytes 6152 | tf_op jit(solution)/shard_map/ppermute | solution.py:187
  18.4 2.4 %copy-start = (s32[2,1024]{1,0:T(2,128)S(1)}, s32[2,1024]{1,0:T(2,128)}, u32[]{:S(2)}) copy-start(s32[2,1024]{1,0:T(2,128)} %bounds_ref.1) | copy-start | bytes 24580
  18.4 2.4 %copy-start.1 = (s32[1024]{0:T(1024)S(1)}, s32[1024]{0:T(1024)}, u32[]{:S(2)}) copy-start(s32[1024]{0:T(1024)} %param.7) | copy-start | bytes 12292
  18.5 6.3 %collective-permute-start.7 = (f32[8,64]{1,0:T(8,128)S(1)}, f32[8,64]{1,0:T(8,128)S(1)}, u32[]{:S(2)}, u32[]{:S(2)}) collective-permute-start(f32[8,64]{1,0:T(8,128)S(1)} %add_select_fusion.1), channel_id=1, source_target_pairs={{0,8},{1,9},{2,10},{3,11},{4,12},{5,13},{6,14},{7,15},{8,0},{9,1},... | collective-permute-start | bytes 6152 | tf_op jit(solution)/shard_map/ppermute | solution.py:187
  20.8 4.1 %collective-permute-start.1 = (f32[64,256]{1,0:T(8,128)S(1)}, f32[64,256]{1,0:T(8,128)S(1)}, u32[]{:S(2)}, u32[]{:S(2)}) collective-permute-start(f32[64,256]{1,0:T(8,128)S(1)} %get-tuple-element.12), channel_id=1, source_target_pairs={{0,1},{1,0},{2,3},{3,2},{4,5},{5,4},{6,7},{7,6},{8,9},{9,8},{10,11... | collective-permute-start | bytes 196616 | tf_op jit(solution)/shard_map/ppermute | solution.py:187
  22.7 5.6 %collective-permute-start.2 = (f32[64,256]{1,0:T(8,128)S(1)}, f32[64,256]{1,0:T(8,128)S(1)}, u32[]{:S(2)}, u32[]{:S(2)}) collective-permute-start(f32[64,256]{1,0:T(8,128)S(1)} %get-tuple-element.13), channel_id=1, source_target_pairs={{1,2},{3,4},{5,6},{7,8},{9,10},{11,12},{13,14},{2,1},{4,3},{6,5},{... | collective-permute-start | bytes 196616 | tf_op jit(solution)/shard_map/ppermute | solution.py:219

commit v3 on v2

--- a/solution.py
+++ b/solution.py
@@ -16,12 +16,45 @@
     return [pl.BlockSpec(memory_space=pltpu.VMEM)] * count
 
 
-def project(components, packed_panel):
+def split(value, upper_ref, lower_ref):
+    rank, columns = value.shape
+    center = jnp.sum(value, axis=1, keepdims=True) * (1.0 / columns)
+    center = center.astype(jnp.bfloat16)
+    rest = value - center.astype(jnp.float32)
+    upper = rest.astype(jnp.bfloat16)
+    upper_ref[:, :columns] = upper
+    upper_ref[:, columns:] = jnp.broadcast_to(center, (rank, LANES))
+    lower_ref[...] = (rest - upper.astype(jnp.float32)).astype(jnp.bfloat16)
+
+
+def pieces(rank, columns):
+    return (
+        jax.ShapeDtypeStruct((rank, columns + LANES), jnp.bfloat16),
+        jax.ShapeDtypeStruct((rank, columns), jnp.bfloat16),
+    )
+
+
+def split_sum(own, other):
+    def kernel(own_ref, other_ref, upper_ref, lower_ref):
+        split(own_ref[...] + other_ref[...], upper_ref, lower_ref)
+
+    return pl.pallas_call(
+        kernel,
+        out_shape=pieces(*own.shape),
+        in_specs=whole_in_vmem(2),
+        out_specs=tuple(whole_in_vmem(2)),
+        compiler_params=pltpu.CompilerParams(vmem_limit_bytes=4 << 20),
+        name="split",
+    )(own, other)
+
+
+def project(components, packed_panel, in_pieces):
     rank, haps = components.shape
     words, columns = packed_panel.shape
     bits = haps // words
 
-    def kernel(panel_ref, components_ref, out_ref, panel, weights_in, turned, arrived):
+    def kernel(panel_ref, components_ref, *refs):
+        outs, (panel, weights_in, turned, product, arrived) = refs[:-5], refs[-5:]
         copies = [
             pltpu.make_async_copy(components_ref, weights_in, arrived.at[0]),
             pltpu.make_async_copy(panel_ref, panel, arrived.at[1]),
@@ -34,25 +67,31 @@
         weights = jnp.concatenate(weights, axis=0).T.astype(jnp.bfloat16)
         copies[1].wait()
         step = min(BLOCK, columns)
+        target = product if in_pieces else outs[0]
         for first in range(0, columns, step):
             packed = panel[:, first : first + step]
             alleles = [
                 (jnp.right_shift(packed, j) & 1).astype(jnp.float32).astype(jnp.bfloat16)
                 for j in range(bits)
             ]
-            out_ref[:, first : first + step] = jnp.dot(
+            target[:, first : first + step] = jnp.dot(
                 weights, jnp.concatenate(alleles, axis=0), preferred_element_type=jnp.float32
             )
-
-    return pl.pallas_call(
-        kernel,
-        out_shape=jax.ShapeDtypeStruct((rank, columns), jnp.float32),
+        if in_pieces:
+            split(product[...], *outs)
+
+    whole = (jax.ShapeDtypeStruct((rank, columns), jnp.float32),)
+    out_shape = pieces(rank, columns) if in_pieces else whole
+    return pl.pallas_call(
+        kernel,
+        out_shape=out_shape,
         in_specs=[pl.BlockSpec(memory_space=pltpu.HBM)] * 2,
-        out_specs=pl.BlockSpec(memory_space=pltpu.VMEM),
+        out_specs=tuple(whole_in_vmem(len(out_shape))),
         scratch_shapes=[
             pltpu.VMEM((words, columns), jnp.int32),
             pltpu.VMEM((rank, haps), jnp.bfloat16),
             pltpu.VMEM((haps, rank), jnp.float32),
+            pltpu.VMEM((rank, columns), jnp.float32),
             pltpu.SemaphoreType.DMA((2,)),
         ],
         compiler_params=pltpu.CompilerParams(vmem_limit_bytes=8 << 20),
@@ -84,37 +123,52 @@
     )(bounds, band_width)
 
 
-def combine(own, other, reach):
-    rank, columns = own.shape
-
-    def kernel(own_ref, other_ref, factor_ref, near_ref, far_ref, moments_ref):
-        odd = lax.rem(lax.axis_index("snp"), 2)
-        factor = own_ref[...] + other_ref[...]
-        factor_ref[...] = factor
+def local_moments(upper, other_upper):
+    rank, columns = upper.shape[0], upper.shape[1] - LANES
+
+    def kernel(own_ref, other_ref, moments_ref):
+        summed = own_ref[...].astype(jnp.float32) + other_ref[...].astype(jnp.float32)
+        center = summed[:, columns:]
+        factor = summed[:, :columns]
         average = jnp.sum(factor, axis=1, keepdims=True) * (1.0 / columns)
         centered = factor - average
         deviation = jnp.sum(centered * centered, axis=1, keepdims=True)
         lane = lax.broadcasted_iota(jnp.int32, (rank, LANES), 1)
-        moments_ref[...] = jnp.where(lane == 0, average, deviation).T[:SUBLANES]
-        low = factor[:, :reach]
-        high = factor[:, columns - reach :]
-        near_ref[...] = jnp.where(odd == 1, low, high)
-        far_ref[...] = jnp.where(odd == 1, high, low)
+        moments_ref[...] = jnp.where(lane == 0, average + center, deviation).T[:SUBLANES]
+
+    return pl.pallas_call(
+        kernel,
+        out_shape=jax.ShapeDtypeStruct((SUBLANES, rank), jnp.float32),
+        in_specs=whole_in_vmem(2),
+        out_specs=pl.BlockSpec(memory_space=pltpu.VMEM),
+        compiler_params=pltpu.CompilerParams(vmem_limit_bytes=4 << 20),
+        name="local_moments",
+    )(upper, other_upper)
+
+
+def whole_factor(upper, other_upper, lower, other_lower, reach):
+    rank, columns = lower.shape
+
+    def kernel(upper_ref, other_upper_ref, lower_ref, other_lower_ref, factor_ref, near_ref, far_ref):
+        odd = lax.rem(lax.axis_index("snp"), 2)
+        high = upper_ref[...].astype(jnp.float32) + other_upper_ref[...].astype(jnp.float32)
+        low = lower_ref[...].astype(jnp.float32) + other_lower_ref[...].astype(jnp.float32)
+        factor = (high[:, :columns] + low) + high[:, columns : columns + 1]
+        factor_ref[...] = factor
+        first = factor[:, :reach]
+        last = factor[:, columns - reach :]
+        near_ref[...] = jnp.where(odd == 1, first, last)
+        far_ref[...] = jnp.where(odd == 1, last, first)
 
     edge = jax.ShapeDtypeStruct((rank, reach), jnp.float32)
     return pl.pallas_call(
         kernel,
-        out_shape=(
-            jax.ShapeDtypeStruct((rank, columns), jnp.float32),
-            edge,
-            edge,
-            jax.ShapeDtypeStruct((SUBLANES, rank), jnp.float32),
-        ),
-        in_specs=whole_in_vmem(2),
-        out_specs=tuple(whole_in_vmem(4)),
+        out_shape=(jax.ShapeDtypeStruct((rank, columns), jnp.float32), edge, edge),
+        in_specs=whole_in_vmem(4),
+        out_specs=tuple(whole_in_vmem(3)),
         compiler_params=pltpu.CompilerParams(vmem_limit_bytes=4 << 20),
-        name="combine",
-    )(own, other)
+        name="whole_factor",
+    )(upper, other_upper, lower, other_lower)
 
 
 def band_scores(factor, near, far, moments, low, high, total):
@@ -207,13 +261,20 @@
     columns = packed_panel.shape[1]
     reach = columns // 4
     devices = lax.axis_size("snp")
-    partial = project(components, packed_panel)
+    hap_steps = powers(lax.axis_size("hap"))
+    parts = project(components, packed_panel, len(hap_steps) == 1)
     low, high = windows(bounds, band_width[None])
-    hap_steps = powers(lax.axis_size("hap"))
     for distance in hap_steps[:-1]:
-        partial = partial + swap(partial, "hap", distance)
-    other = swap(partial, "hap", hap_steps[-1])
-    factor, near, far, moments = combine(partial, other, reach)
+        other = swap(parts[0], "hap", distance)
+        if distance == hap_steps[-2]:
+            parts = split_sum(parts[0], other)
+        else:
+            parts = (parts[0] + other,)
+    upper, lower = parts
+    other_upper = swap(upper, "hap", hap_steps[-1])
+    other_lower = swap(lower, "hap", hap_steps[-1])
+    moments = local_moments(upper, other_upper)
+    factor, near, far = whole_factor(upper, other_upper, lower, other_lower, reach)
     outward = [(i, i + 1) for i in range(1, devices - 1, 2)]
     near = swap(near, "snp", 1)
     far = lax.ppermute(far, "snp", outward + [(j, i) for i, j in outward])

time: 30.5 us -> 28.1 us (0.921)
  waiting for transfers between devices: 13.3 us -> 9.37 us
  starting transfers between devices: 12.6 us -> 13.9 us
    ppermute x7 -> x8, waiting for transfers between devices: 9.98 us -> 6.46 us  [swap(): return lax.ppermute(value, axis, [(i, i ^ distance) for i in range(count)])]
    ppermute x7 -> x8, starting transfers between devices: 10.5 us -> 11.4 us  [swap(): return lax.ppermute(value, axis, [(i, i ^ distance) for i in range(count)])]
    ppermute x1, starting transfers between devices: 2.11 us -> 2.49 us  [on_device(): far = lax.ppermute(far, 'snp', outward + [(j, i) for i, j in outward])]
    ppermute x1, waiting for transfers between devices: 3.28 us -> 2.91 us  [on_device(): far = lax.ppermute(far, 'snp', outward + [(j, i) for i, j in outward])]
    pallas_call x2 -> x3, Pallas kernels: 1.88 us -> 2.09 us  [the longest x1 1.74 us: project(): pl.pallas_call(kernel, out_shape=out_shape, in_specs=[pl.BlockSpec(memory...]
  transfers between devices with their start and end apart: 8 -> 9, of which waited for: 5 -> 5; matrix products, arithmetic and copies ran while one was open for 1% -> 1% of each run, Pallas kernels for 0% -> 0%
where the time goes in v3:
time: 28.1 us; the launch traced here: 27.9 us
  starting transfers between devices  13.9 us (49%)
  waiting for transfers between devices  9.37 us (33%)
  Pallas kernels  4.2 us (15%)
  other arithmetic  0.41 us (1%)
    ppermute x8, starting transfers between devices, swap(): return lax.ppermute(value, axis, [(i, i ^ distance) for i in range(count)])  11.4 us
    ppermute x8, waiting for transfers between devices, swap(): return lax.ppermute(value, axis, [(i, i ^ distance) for i in range(count)])  6.46 us
    ppermute x1, waiting for transfers between devices, on_device(): far = lax.ppermute(far, 'snp', outward + [(j, i) for i, j in outward])  2.91 us
    ppermute x1, starting transfers between devices, on_device(): far = lax.ppermute(far, 'snp', outward + [(j, i) for i, j in outward])  2.49 us
    pallas_call x1, Pallas kernels, band_scores(): pl.pallas_call(kernel, out_shape=jax.ShapeDtypeStruct((1, columns), jnp.f...  2.09 us
    pallas_call x1, Pallas kernels, project(): pl.pallas_call(kernel, out_shape=out_shape, in_specs=[pl.BlockSpec(memory...  1.74 us
  transfers between devices with their start and end apart: 9, of which 5 were waited for; matrix products, arithmetic and copies ran while one was open for 1% of the time, Pallas kernels for 0%

profile of v3, /device:TPU:1, one launch (start us, length us, event | category | flops | bytes accessed | tf_op | source)
XLA Modules:
  0.0 27.9 jit_solution(14603403874141209174)
XLA Ops:
  0.0 1.7 %project.1 = (bf16[64,1152]{1,0:T(8,128)(2,1)S(1)}, bf16[64,1024]{1,0:T(8,128)(2,1)S(1)}) custom-call(s32[48,1024]{1,0:T(8,128)} %panel_ref.1, bf16[64,624]{1,0:T(8,128)(2,1)} %components_ref.1), custom_call_target="tpu_custom_call" | custom-call | tf_op jit(solution)/shard_map/project/pallas_call | solution.py:85
  1.7 2.1 %collective-permute-start = (bf16[64,1152]{1,0:T(8,128)(2,1)S(1)}, bf16[64,1152]{1,0:T(8,128)(2,1)S(1)}, u32[]{:S(2)}, u32[]{:S(2)}) collective-permute-start(bf16[64,1152]{1,0:T(8,128)(2,1)S(1)} %get-tuple-element.12.upper_ref.own_ref), channel_id=1, source_target_pairs={{0,16},{16,0},{1,17},{17,1},{2,18},{18,2},{3,19},{19,3},{4,20},{20... | collective-permute-start | bytes 442376 | tf_op jit(solution)/shard_map/ppermute | solution.py:241
  3.8 3.6 %collective-permute-done.other_upper_ref.other_ref = bf16[64,1152]{1,0:T(8,128)(2,1)S(1)} collective-permute-done((bf16[64,1152]{1,0:T(8,128)(2,1)S(1)}, bf16[64,1152]{1,0:T(8,128)(2,1)S(1)}, u32[]{:S(2)}, u32[]{:S(2)}) %collective-permute-start) | collective-permute-done | bytes 147488 | tf_op jit(solution)/shard_map/ppermute | solution.py:241
  7.4 0.2 local_moments.1
  7.6 2.6 %collective-permute-start.6 = (f32[8,64]{1,0:T(8,128)S(1)}, f32[8,64]{1,0:T(8,128)S(1)}, u32[]{:S(2)}, u32[]{:S(2)}) collective-permute-start(f32[8,64]{1,0:T(8,128)S(1)} %local_moments.1), channel_id=1, source_target_pairs={{0,3},{1,2},{2,1},{3,0},{4,7},{5,6},{6,5},{7,4},{8,11},{9,10},{10,... | collective-permute-start | bytes 6152 | tf_op jit(solution)/shard_map/ppermute | solution.py:241
  10.3 0.0 collective-permute-start.5
  10.3 0.5 %collective-permute-start.4 = (f32[8,64]{1,0:T(8,128)S(1)}, f32[8,64]{1,0:T(8,128)S(1)}, u32[]{:S(2)}, u32[]{:S(2)}) collective-permute-start(f32[8,64]{1,0:T(8,128)S(1)} %local_moments.1), channel_id=1, source_target_pairs={{0,1},{1,0},{2,3},{3,2},{4,5},{5,4},{6,7},{7,6},{8,9},{9,8},{10,11... | collective-permute-start | bytes 6152 | tf_op jit(solution)/shard_map/ppermute | solution.py:241
  10.8 0.8 %collective-permute-done.6 = f32[8,64]{1,0:T(8,128)S(1)} collective-permute-done((f32[8,64]{1,0:T(8,128)S(1)}, f32[8,64]{1,0:T(8,128)S(1)}, u32[]{:S(2)}, u32[]{:S(2)}) %collective-permute-start.6) | collective-permute-done | bytes 2080 | tf_op jit(solution)/shard_map/ppermute | solution.py:241
  11.6 1.2 %collective-permute-done.5 = f32[8,64]{1,0:T(8,128)S(1)} collective-permute-done((f32[8,64]{1,0:T(8,128)S(1)}, f32[8,64]{1,0:T(8,128)S(1)}, u32[]{:S(2)}, u32[]{:S(2)}) %collective-permute-start.5) | collective-permute-done | bytes 2080 | tf_op jit(solution)/shard_map/ppermute | solution.py:241
  12.7 0.0 collective-permute-done.4
  12.8 0.1 add_select_fusion.2
  12.8 1.3 %collective-permute-start.7 = (f32[8,64]{1,0:T(8,128)S(1)}, f32[8,64]{1,0:T(8,128)S(1)}, u32[]{:S(2)}, u32[]{:S(2)}) collective-permute-start(f32[8,64]{1,0:T(8,128)S(1)} %add_select_fusion.2), channel_id=1, source_target_pairs={{0,4},{1,5},{2,6},{3,7},{4,0},{5,1},{6,2},{7,3},{8,12},{9,13},{10,... | collective-permute-start | bytes 6152 | tf_op jit(solution)/shard_map/ppermute | solution.py:241
  14.1 1.2 %collective-permute-start.1 = (bf16[64,1024]{1,0:T(8,128)(2,1)S(1)}, bf16[64,1024]{1,0:T(8,128)(2,1)S(1)}, u32[]{:S(2)}, u32[]{:S(2)}) collective-permute-start(bf16[64,1024]{1,0:T(8,128)(2,1)S(1)} %get-tuple-element.13.lower_ref), channel_id=1, source_target_pairs={{0,16},{16,0},{1,17},{17,1},{2,18},{18,2},{3,19},{19,3},{4,20},{20... | collective-permute-start | bytes 393224 | tf_op jit(solution)/shard_map/ppermute | solution.py:241
  15.4 0.0 collective-permute-done.7
  15.4 0.1 fusion.1
  15.4 0.0 copy-start
  15.4 0.0 copy-start.1
  15.5 0.1 add_select_fusion.1
  15.5 2.3 %collective-permute-start.8 = (f32[8,64]{1,0:T(8,128)S(1)}, f32[8,64]{1,0:T(8,128)S(1)}, u32[]{:S(2)}, u32[]{:S(2)}) collective-permute-start(f32[8,64]{1,0:T(8,128)S(1)} %add_select_fusion.1), channel_id=1, source_target_pairs={{0,8},{1,9},{2,10},{3,11},{4,12},{5,13},{6,14},{7,15},{8,0},{9,1},... | collective-permute-start | bytes 6152 | tf_op jit(solution)/shard_map/ppermute | solution.py:241
  17.8 0.0 copy-done
  17.8 0.0 copy-done.1
  17.9 0.9 %collective-permute-done.1.other_lower_ref = bf16[64,1024]{1,0:T(8,128)(2,1)S(1)} collective-permute-done((bf16[64,1024]{1,0:T(8,128)(2,1)S(1)}, bf16[64,1024]{1,0:T(8,128)(2,1)S(1)}, u32[]{:S(2)}, u32[]{:S(2)}) %collective-permute-start.1) | collective-permute-done | bytes 131104 | tf_op jit(solution)/shard_map/ppermute | solution.py:241
  18.8 0.1 whole_factor.1
  18.9 1.3 %collective-permute-start.2 = (f32[64,256]{1,0:T(8,128)S(1)}, f32[64,256]{1,0:T(8,128)S(1)}, u32[]{:S(2)}, u32[]{:S(2)}) collective-permute-start(f32[64,256]{1,0:T(8,128)S(1)} %get-tuple-element.15), channel_id=1, source_target_pairs={{0,1},{1,0},{2,3},{3,2},{4,5},{5,4},{6,7},{7,6},{8,9},{9,8},{10,11... | collective-permute-start | bytes 196616 | tf_op jit(solution)/shard_map/ppermute | solution.py:241
  20.2 2.5 %collective-permute-start.3 = (f32[64,256]{1,0:T(8,128)S(1)}, f32[64,256]{1,0:T(8,128)S(1)}, u32[]{:S(2)}, u32[]{:S(2)}) collective-permute-start(f32[64,256]{1,0:T(8,128)S(1)} %get-tuple-element.16), channel_id=1, source_target_pairs={{1,2},{3,4},{5,6},{7,8},{9,10},{11,12},{13,14},{2,1},{4,3},{6,5},{... | collective-permute-start | bytes 196616 | tf_op jit(solution)/shard_map/ppermute | solution.py:280
  22.7 0.0 collective-permute-done.8
  22.7 0.1 fusion
  22.8 0.1 add_select_fusion.moments_ref
  22.9 0.0 collective-permute-done.2.near_ref
  22.9 2.9 %collective-permute-done.3.far_ref = f32[64,256]{1,0:T(8,128)S(1)} collective-permute-done((f32[64,256]{1,0:T(8,128)S(1)}, f32[64,256]{1,0:T(8,128)S(1)}, u32[]{:S(2)}, u32[]{:S(2)}) %collective-permute-start.3) | collective-permute-done | bytes 65568 | tf_op jit(solution)/shard_map/ppermute | solution.py:280
  25.8 2.1 %band.1 = f32[1,1024]{1,0:T(1,128)} custom-call(f32[64,1024]{1,0:T(8,128)S(1)} %get-tuple-element.14.factor_ref, f32[64,256]{1,0:T(8,128)S(1)} %collective-permute-done.2.near_ref, f32[64,256]{1,0:T(8,128)S(1)} %collective-permute-done.3.far_ref, f32[8,64]{1,0:T(8,128)S(1)} %add_select_fusion.moments_ref, s32[1,1024]{1,0:T(1,128)S(1)} %get-tuple-element.17.low_ref, ...), custom_call_target="tpu_custom_call" | custom-call | tf_op jit(solution)/shard_map/band/pallas_call | solution.py:224
  (6 shorter events, 0.1 us)
Async XLA Ops:
  1.7 5.6 %collective-permute-start = (bf16[64,1152]{1,0:T(8,128)(2,1)S(1)}, bf16[64,1152]{1,0:T(8,128)(2,1)S(1)}, u32[]{:S(2)}, u32[]{:S(2)}) collective-permute-start(bf16[64,1152]{1,0:T(8,128)(2,1)S(1)} %get-tuple-element.12.upper_ref.own_ref), channel_id=1, source_target_pairs={{0,16},{16,0},{1,17},{17,1},{2,18},{18,2},{3,19},{19,3},{4,20},{20... | collective-permute-start | bytes 442376 | tf_op jit(solution)/shard_map/ppermute | solution.py:241
  7.6 3.9 %collective-permute-start.6 = (f32[8,64]{1,0:T(8,128)S(1)}, f32[8,64]{1,0:T(8,128)S(1)}, u32[]{:S(2)}, u32[]{:S(2)}) collective-permute-start(f32[8,64]{1,0:T(8,128)S(1)} %local_moments.1), channel_id=1, source_target_pairs={{0,3},{1,2},{2,1},{3,0},{4,7},{5,6},{6,5},{7,4},{8,11},{9,10},{10,... | collective-permute-start | bytes 6152 | tf_op jit(solution)/shard_map/ppermute | solution.py:241
  10.3 2.5 %collective-permute-start.5 = (f32[8,64]{1,0:T(8,128)S(1)}, f32[8,64]{1,0:T(8,128)S(1)}, u32[]{:S(2)}, u32[]{:S(2)}) collective-permute-start(f32[8,64]{1,0:T(8,128)S(1)} %local_moments.1), channel_id=1, source_target_pairs={{0,2},{1,3},{2,0},{3,1},{4,6},{5,7},{6,4},{7,5},{8,10},{9,11},{10,... | collective-permute-start | bytes 6152 | tf_op jit(solution)/shard_map/ppermute | solution.py:241
  10.3 2.5 %collective-permute-start.4 = (f32[8,64]{1,0:T(8,128)S(1)}, f32[8,64]{1,0:T(8,128)S(1)}, u32[]{:S(2)}, u32[]{:S(2)}) collective-permute-start(f32[8,64]{1,0:T(8,128)S(1)} %local_moments.1), channel_id=1, source_target_pairs={{0,1},{1,0},{2,3},{3,2},{4,5},{5,4},{6,7},{7,6},{8,9},{9,8},{10,11... | collective-permute-start | bytes 6152 | tf_op jit(solution)/shard_map/ppermute | solution.py:241
  12.8 2.5 %collective-permute-start.7 = (f32[8,64]{1,0:T(8,128)S(1)}, f32[8,64]{1,0:T(8,128)S(1)}, u32[]{:S(2)}, u32[]{:S(2)}) collective-permute-start(f32[8,64]{1,0:T(8,128)S(1)} %add_select_fusion.2), channel_id=1, source_target_pairs={{0,4},{1,5},{2,6},{3,7},{4,0},{5,1},{6,2},{7,3},{8,12},{9,13},{10,... | collective-permute-start | bytes 6152 | tf_op jit(solution)/shard_map/ppermute | solution.py:241
  14.1 4.6 %collective-permute-start.1 = (bf16[64,1024]{1,0:T(8,128)(2,1)S(1)}, bf16[64,1024]{1,0:T(8,128)(2,1)S(1)}, u32[]{:S(2)}, u32[]{:S(2)}) collective-permute-start(bf16[64,1024]{1,0:T(8,128)(2,1)S(1)} %get-tuple-element.13.lower_ref), channel_id=1, source_target_pairs={{0,16},{16,0},{1,17},{17,1},{2,18},{18,2},{3,19},{19,3},{4,20},{20... | collective-permute-start | bytes 393224 | tf_op jit(solution)/shard_map/ppermute | solution.py:241
  15.4 2.4 %copy-start = (s32[2,1024]{1,0:T(2,128)S(1)}, s32[2,1024]{1,0:T(2,128)}, u32[]{:S(2)}) copy-start(s32[2,1024]{1,0:T(2,128)} %bounds_ref.1) | copy-start | bytes 24580
  15.4 2.4 %copy-start.1 = (s32[1024]{0:T(1024)S(1)}, s32[1024]{0:T(1024)}, u32[]{:S(2)}) copy-start(s32[1024]{0:T(1024)} %param.7) | copy-start | bytes 12292
  15.5 7.2 %collective-permute-start.8 = (f32[8,64]{1,0:T(8,128)S(1)}, f32[8,64]{1,0:T(8,128)S(1)}, u32[]{:S(2)}, u32[]{:S(2)}) collective-permute-start(f32[8,64]{1,0:T(8,128)S(1)} %add_select_fusion.1), channel_id=1, source_target_pairs={{0,8},{1,9},{2,10},{3,11},{4,12},{5,13},{6,14},{7,15},{8,0},{9,1},... | collective-permute-start | bytes 6152 | tf_op jit(solution)/shard_map/ppermute | solution.py:241
  18.9 4.0 %collective-permute-start.2 = (f32[64,256]{1,0:T(8,128)S(1)}, f32[64,256]{1,0:T(8,128)S(1)}, u32[]{:S(2)}, u32[]{:S(2)}) collective-permute-start(f32[64,256]{1,0:T(8,128)S(1)} %get-tuple-element.15), channel_id=1, source_target_pairs={{0,1},{1,0},{2,3},{3,2},{4,5},{5,4},{6,7},{7,6},{8,9},{9,8},{10,11... | collective-permute-start | bytes 196616 | tf_op jit(solution)/shard_map/ppermute | solution.py:241
  20.2 5.6 %collective-permute-start.3 = (f32[64,256]{1,0:T(8,128)S(1)}, f32[64,256]{1,0:T(8,128)S(1)}, u32[]{:S(2)}, u32[]{:S(2)}) collective-permute-start(f32[64,256]{1,0:T(8,128)S(1)} %get-tuple-element.16), channel_id=1, source_target_pairs={{1,2},{3,4},{5,6},{7,8},{9,10},{11,12},{13,14},{2,1},{4,3},{6,5},{... | collective-permute-start | bytes 196616 | tf_op jit(solution)/shard_map/ppermute | solution.py:280
